TPU v7x, 256 devices: a whole 4x4x8 slice. The times are simulated.
256 devices in a mesh: stream: 2 (over z_hi), dp: 16 (over x, y), tensor: 8 (over z_lo, core).
Axes of the slice: x: 4, y: 4, z: 8 (z_hi: 2, z_lo: 4; z = z_hi * 4 + z_lo), core: 2. Of those that a mesh axis runs over, the one named last changes fastest.
Arguments:
- hidden: bfloat16 [2, 256, 8192], P('stream', 'tensor', 'dp'), may hold values from -3 to 3
- cached_rotated_keys: bfloat16 [2, 256, 8, 256, 128], P('stream', 'dp', 'tensor'), may hold values from -6 to 6
- cached_values: bfloat16 [2, 256, 8, 256, 128], P('stream', 'dp', 'tensor'), may hold values from -18 to 18
- cache_lengths: int32 [2, 256], P('stream', 'dp'), may hold values from 1 to 256, as said below
- recent_ids: int32 [256, 128], replicated, may hold values from 0 to 65535
- guidance: float32 [256], replicated, may hold values from 1 to 3
- w_query: bfloat16 [8192, 8192], P('dp', 'tensor'), may hold values from -0.0625 to 0.0625
- key_value_weight: bfloat16 [8192, 2, 1024], P('dp', None, 'tensor'), may hold values from -0.0625 to 0.0625
- w_output: bfloat16 [8192, 8192], P('tensor', 'dp'), may hold values from -0.0625 to 0.0625
- norm_gain: bfloat16 [8192], P('dp'), may hold values from 0.5 to 1.5
- w_head: bfloat16 [8192, 65536], P(None, ('dp', 'tensor')), may hold values from -0.16503906 to 0.16503906
Outputs:
- guided_logprobs: float32 [256, 65536], P('stream', ('dp', 'tensor'))
Inputs may be any that keep to these rules, and one draw needn't show every extreme that they name: `cache_lengths`: every prompt has 1 to 256 filled slots in each stream; some prompt has all 256; lengths differ widely from one group of 16 prompts to the next.
All inputs are finite; a program needn't handle non-finite values.
Results may differ from a plain program's by a relative error of at most 0.0025.
Values may be sent and summed in bfloat16 or wider, within the bound.
A program may use at most 64 MiB of HBM per device.

v0:
```python
import jax
import jax.numpy as jnp
from jax import lax
from jax.sharding import PartitionSpec as P

MODEL_WIDTH = 8192
HEAD_SIZE = 128
rope_theta = 500000.0
penalty_step = 1.5
norm_eps = 1e-05


def partner_2(value, axis, distance):
    mask = 2**distance
    pairs = [(source, source ^ mask) for source in range(lax.axis_size(axis))]
    return lax.ppermute(value, axis, pairs)


def rotate(values, positions):
    halfway = values.shape[-1] // 2
    frequency = rope_theta ** (-(jnp.arange(halfway, dtype=jnp.float32) * 2.0 / values.shape[-1]))
    angles = positions.astype(jnp.float32)[:, None, None] * frequency
    cosine_term = jnp.cos(angles)
    sine_term = jnp.sin(angles)
    first_half = values[..., :halfway]
    second_half = values[..., halfway:]
    return jnp.concatenate(
        [
            first_half * cosine_term - second_half * sine_term,
            second_half * cosine_term + first_half * sine_term,
        ],
        axis=-1,
    )


def repeat_counts(recent_ids, first_column, width):
    columns = first_column + jnp.arange(width, dtype=jnp.int32)
    return jnp.sum((recent_ids[:, :, None] == columns[None, None, :]).astype(jnp.float32), 1)


def body(
    hidden,
    cached_rotated_keys,
    cached_values,
    cache_lengths,
    recent_ids,
    guidance,
    w_query,
    key_value_weight,
    w_output,
    norm_gain,
    w_head,
):
    local_width = hidden.shape[2]
    query_cols = w_query.shape[1]
    kv_cols = key_value_weight.shape[2]
    local_prompts = cache_lengths.shape[1]
    lengths = cache_lengths[0]
    vocab_local = w_head.shape[1]
    all_rows = lax.all_gather(hidden[0], "tensor", axis=0, tiled=True)
    kv_flat = key_value_weight.reshape(local_width, 2 * kv_cols)
    projected = lax.psum_scatter(
        jnp.concatenate(
            [
                jnp.dot(all_rows, w_query, preferred_element_type=jnp.float32),
                jnp.dot(all_rows, kv_flat, preferred_element_type=jnp.float32),
            ],
            axis=1,
        ),
        "dp",
        scatter_dimension=0,
        tiled=True,
    )
    query_heads = query_cols // HEAD_SIZE
    kv_heads = kv_cols // HEAD_SIZE
    rotated_query = rotate(
        projected[:, :query_cols].reshape(local_prompts, query_heads, HEAD_SIZE), lengths
    ).astype(jnp.bfloat16)
    key_value_rows = projected[:, query_cols:].reshape(local_prompts, 2, kv_heads, HEAD_SIZE)
    fresh_key = rotate(key_value_rows[:, 0], lengths).astype(jnp.bfloat16)
    value_new = key_value_rows[:, 1].astype(jnp.bfloat16)
    grouped_queries = rotated_query.reshape(
        local_prompts, kv_heads, query_heads // kv_heads, HEAD_SIZE
    )
    attention_scale = HEAD_SIZE ** (-0.5)
    key_block = cached_rotated_keys[0]
    value_block = cached_values[0]
    scores = (
        jnp.einsum(
            "pkgd,pksd->pkgs", grouped_queries, key_block, preferred_element_type=jnp.float32
        )
        * attention_scale
    )
    self_score = (
        jnp.einsum("pkgd,pkd->pkg", grouped_queries, fresh_key, preferred_element_type=jnp.float32)
        * attention_scale
    )
    valid = jnp.arange(key_block.shape[2], dtype=jnp.int32)[None, :] < lengths[:, None]
    exps = jnp.where(valid[:, None, None, :], jnp.exp(scores), 0.0)
    own_exp = jnp.exp(self_score)
    denominator = jnp.sum(exps, -1) + own_exp
    weights = (exps / denominator[..., None]).astype(jnp.bfloat16)
    own_weight = (own_exp / denominator).astype(jnp.bfloat16)
    attended = jnp.einsum(
        "pkgs,pksd->pkgd", weights, value_block, preferred_element_type=jnp.float32
    )
    attended = (
        attended
        + own_weight.astype(jnp.float32)[..., None] * value_new.astype(jnp.float32)[:, :, None, :]
    )
    attended = attended.reshape(local_prompts, query_cols).astype(jnp.bfloat16)
    partial_out = jnp.dot(
        lax.all_gather(attended, "dp", axis=0, tiled=True),
        w_output,
        preferred_element_type=jnp.float32,
    )
    output_sum = lax.psum_scatter(partial_out, "tensor", scatter_dimension=0, tiled=True)
    residual = (hidden[0].astype(jnp.float32) + output_sum).astype(jnp.bfloat16)
    widened = residual.astype(jnp.float32)
    squares = lax.psum(jnp.sum(widened * widened, 1), "dp")
    inverse = lax.rsqrt(squares / MODEL_WIDTH + norm_eps)
    normed = (widened * inverse[:, None] * norm_gain.astype(jnp.float32)).astype(jnp.bfloat16)
    normed_all = lax.all_gather(normed, "tensor", axis=0, tiled=True)
    logits = jnp.dot(
        lax.all_gather(normed_all, "dp", axis=1, tiled=True),
        w_head,
        preferred_element_type=jnp.float32,
    )
    stream_side = lax.axis_index("stream")
    half_rows = logits.shape[0] // 2
    mine_start = stream_side * half_rows
    other_start = (1 - stream_side) * half_rows
    column_base = lax.axis_index(("dp", "tensor")) * vocab_local
    mine = lax.dynamic_slice_in_dim(logits, mine_start, half_rows, 0)
    sending = lax.dynamic_slice_in_dim(logits, other_start, half_rows, 0)
    partner = partner_2(sending, "stream", 0)
    conditional = jnp.where(stream_side == 0, mine, partner)
    unconditional = jnp.where(stream_side == 0, partner, mine)
    guide = lax.dynamic_slice_in_dim(guidance, mine_start, half_rows, 0)[:, None]
    recent_mine = lax.dynamic_slice_in_dim(recent_ids, mine_start, half_rows, 0)
    guided = unconditional + guide * (conditional - unconditional)
    guided = guided - penalty_step * repeat_counts(recent_mine, column_base, vocab_local)
    totals = lax.psum(jnp.sum(jnp.exp(guided), 1), ("dp", "tensor"))
    return guided - jnp.log(totals)[:, None]


def solution(mesh):
    return jax.shard_map(
        body,
        mesh=mesh,
        in_specs=(
            P("stream", "tensor", "dp"),
            P("stream", "dp", "tensor", None, None),
            P("stream", "dp", "tensor", None, None),
            P("stream", "dp"),
            P(),
            P(),
            P("dp", "tensor"),
            P("dp", None, "tensor"),
            P("tensor", "dp"),
            P("dp"),
            P(None, ("dp", "tensor")),
        ),
        out_specs=P("stream", ("dp", "tensor")),
        check_vma=False,
    )
```

profile of v0, /device:TPU:128, one launch (start us, length us, event | category | flops | bytes accessed | tf_op | source)
XLA Modules:
  0.0 647.4 jit_solution(1154850240006349418)
XLA Ops:
  6.6 14.5 %all-gather = bf16[1,256,512]{2,1,0:T(8,128)(2,1)S(1)} all-gather(bf16[1,32,512]{2,1,0:T(8,128)(2,1)} %param.11), channel_id=2, replica_groups=mesh['stream'=2,'dp'=16,'tensor'=8] {'tensor'}, dimensions={1}, use_global_device_ids=true | all-gather | bytes 294912 | tf_op jit(solution)/shard_map/all_gather | solution.py:60
  21.1 0.5 fusion.9
  21.6 1.2 fusion.5
  22.8 1.2 pad_maximum_fusion
  24.1 0.7 bitcast_convert_fusion
  24.7 0.7 iota_compare_fusion
  25.6 79.2 %reduce-scatter.3.cloned.1.call-done = f32[16,1280]{1,0:T(8,128)} async-done(((f32[256,1280]{1,0:T(8,128)}), f32[16,1280]{1,0:T(8,128)}) %reduce-scatter.3.cloned.1.call-update) | async-done | bytes 81936 | tf_op jit(solution)/shard_map/reduce_scatter | solution.py:62
  104.8 0.7 slice.36
  105.7 0.8 slice_bitcast_fusion
  106.9 1.7 fusion.33
  108.7 0.3 fusion.2
  109.0 23.3 %all_gather.13 = bf16[256,1024]{1,0:T(8,128)(2,1)S(1)} all-gather(bf16[16,1024]{1,0:T(8,128)(2,1)S(1)} %bitcast.51), channel_id=1, replica_groups=mesh['stream'=2,'dp'=16,'tensor'=8] {'dp'}, dimensions={0}, use_global_device_ids=true | all-gather | bytes 557056 | tf_op jit(solution)/shard_map/all_gather | solution.py:113
  132.3 1.2 fusion.34
  133.6 32.9 %reduce-scatter.5.cloned.1.call-done = f32[32,512]{1,0:T(8,128)} async-done(((f32[256,512]{1,0:T(8,128)}), f32[32,512]{1,0:T(8,128)}) %reduce-scatter.5.cloned.1.call-update) | async-done | bytes 65552 | tf_op jit(solution)/shard_map/reduce_scatter | solution.py:117
  166.5 1.0 fusion.11
  167.5 40.3 %psum.14 = f32[32]{0:T(128)S(1)} all-reduce(f32[32]{0:T(128)S(1)} %fusion.11), channel_id=1, replica_groups=mesh['stream'=2,'dp'=16,'tensor'=8] {'dp'}, use_global_device_ids=true, to_apply=%region_4.5 | all-reduce | flops 32 | bytes 256 | tf_op jit(solution)/shard_map/psum | solution.py:120
  207.8 0.9 fusion.13
  208.7 15.3 %all_gather.14 = bf16[256,512]{1,0:T(8,128)(2,1)} all-gather(bf16[32,512]{1,0:T(8,128)(2,1)S(1)} %fusion.13), channel_id=1, replica_groups=mesh['stream'=2,'dp'=16,'tensor'=8] {'tensor'}, dimensions={0}, use_global_device_ids=true | all-gather | bytes 294912 | tf_op jit(solution)/shard_map/all_gather | solution.py:123
  224.2 58.3 %all-gather.3.cloned.1.call-done = bf16[256,8192]{1,0:T(8,128)(2,1)} async-done(((bf16[256,512]{1,0:T(8,128)(2,1)}), bf16[256,8192]{1,0:T(8,128)(2,1)}) %all-gather.3.cloned.1.call-update) | async-done | bytes 4194320 | tf_op jit(solution)/shard_map/all_gather | solution.py:125
  282.5 7.0 %fusion.35 = f32[256,512]{1,0:T(8,128)S(1)} fusion(bf16[256,8192]{1,0:T(8,128)(2,1)} %all-gather.3.cloned.1.call-done, bf16[8192,512]{1,0:T(8,128)(2,1)} %param.21), kind=kOutput, calls=%fused_computation.66 | convolution fusion | flops 2147483648 | bytes 13107200 | tf_op jit(solution)/shard_map/dot_general | solution.py:124
  289.8 4.7 convert_reduce_fusion
  294.4 11.4 %collective-permute-done = f32[128,512]{1,0:T(8,128)S(1)} collective-permute-done((f32[128,512]{1,0:T(8,128)S(1)}, f32[128,512]{1,0:T(8,128)S(1)}, u32[]{:S(2)}, u32[]{:S(2)}) %collective-permute-start) | collective-permute-done | bytes 262176 | tf_op jit(solution)/shard_map/ppermute | solution.py:16
  306.0 334.1 %psum.15 = f32[128]{0:T(128)S(1)} all-reduce(f32[128]{0:T(128)S(1)} %get-tuple-element.5), channel_id=1, replica_groups=mesh['stream'=2,'dp'=16,'tensor'=8] {'dp','tensor'}, use_global_device_ids=true, to_apply=%region_7.8 | all-reduce | flops 128 | bytes 1024 | tf_op jit(solution)/shard_map/psum | solution.py:143
  640.1 0.8 broadcast_subtract_fusion
  (41 shorter events, 1.5 us)
Async XLA Ops:
  6.5 14.6 %copy-start = (bf16[512,1024]{1,0:T(8,128)(2,1)S(1)}, bf16[512,1024]{1,0:T(8,128)(2,1)}, u32[]{:S(2)}) copy-start(bf16[512,1024]{1,0:T(8,128)(2,1)} %param.17) | copy-start | bytes 3145732
  6.5 160.0 %copy-start.3 = (bf16[1,32,512]{2,1,0:T(8,128)(2,1)S(1)}, bf16[1,32,512]{2,1,0:T(8,128)(2,1)}, u32[]{:S(2)}) copy-start(bf16[1,32,512]{2,1,0:T(8,128)(2,1)} %param.11) | copy-start | bytes 98308
  6.5 102.2 %copy-start.1 = (bf16[1,16,1,256,128]{4,3,2,1,0:T(8,128)(2,1)S(1)}, bf16[1,16,1,256,128]{4,3,2,1,0:T(8,128)(2,1)}, u32[]{:S(2)}) copy-start(bf16[1,16,1,256,128]{4,3,2,1,0:T(8,128)(2,1)} %param.13) | copy-start | bytes 3145732
  6.5 125.8 %copy-start.2 = (bf16[1024,512]{1,0:T(8,128)(2,1)S(1)}, bf16[1024,512]{1,0:T(8,128)(2,1)}, u32[]{:S(2)}) copy-start(bf16[1024,512]{1,0:T(8,128)(2,1)} %param.19) | copy-start | bytes 3145732
  6.5 127.1 %copy-start.5 = (bf16[512]{0:T(512)(128)(2,1)S(1)}, bf16[512]{0:T(512)(128)(2,1)}, u32[]{:S(2)}) copy-start(bf16[512]{0:T(512)(128)(2,1)} %param.20) | copy-start | bytes 3076
  6.5 217.5 %copy-start.6 = (f32[256]{0:T(256)S(1)}, f32[256]{0:T(256)}, u32[]{:S(2)}) copy-start(f32[256]{0:T(256)} %param.16) | copy-start | bytes 3076
  6.6 217.6 %copy-start.4 = (s32[256,128]{1,0:T(8,128)S(1)}, s32[256,128]{1,0:T(8,128)}, u32[]{:S(2)}) copy-start(s32[256,128]{1,0:T(8,128)} %param.15) | copy-start | bytes 393220
  6.6 98.2 %reduce-scatter.3.cloned.1.call-start = ((), (), s32[]{:S(2)}) async-start(), calls=%async_computation.2 | async-start | bytes 1392640 | tf_op jit(solution)/shard_map/reduce_scatter | solution.py:62
  24.0 142.5 %reduce-scatter.5.cloned.1.call-start = ((), (), s32[]{:S(2)}) async-start(), calls=%async_computation.3 | async-start | bytes 589824 | tf_op jit(solution)/shard_map/reduce_scatter | solution.py:117
  133.6 148.9 %all-gather.3.cloned.1.call-start = ((), (), s32[]{:S(2)}) async-start(), calls=%async_computation.4 | async-start | bytes 4456448 | tf_op jit(solution)/shard_map/all_gather | solution.py:125
  289.5 16.3 %collective-permute-start = (f32[128,512]{1,0:T(8,128)S(1)}, f32[128,512]{1,0:T(8,128)S(1)}, u32[]{:S(2)}, u32[]{:S(2)}) collective-permute-start(f32[128,512]{1,0:T(8,128)S(1)} %constant_dynamic-slice_fusion.1), channel_id=1, source_target_pairs={{0,128},{128,0},{1,129},{129,1},{2,130},{130,2},{3,131},{131,3},{4... | collective-permute-start | bytes 786440 | tf_op jit(solution)/shard_map/ppermute | solution.py:16
Sparse Core Ops, SparseCore 0:
  24.1 80.6 reduce-scatter.2
  133.7 32.7 reduce-scatter.4
  224.2 58.2 all-gather.2
where the time goes:
time: 648 us; the launch traced here: 647 us
  blocking collectives  427 us (66%)
  waiting for transfers between devices  182 us (28%)
  between operations  13.3 us (2%)
  matrix products  12.1 us (2%)
  other arithmetic  10.5 us (2%)
    psum x1, blocking collectives, body(): totals = lax.psum(jnp.sum(jnp.exp(guided), 1), ('dp', 'tensor'))  334 us
    reduce_scatter x1, waiting for transfers between devices, body(): lax.psum_scatter(jnp.concatenate([jnp.dot(all_rows, w_query, preferred_el...  79.2 us
    all_gather x1, waiting for transfers between devices, body(): lax.all_gather(normed_all, 'dp', axis=1, tiled=True)  58.3 us
    psum x1, blocking collectives, body(): squares = lax.psum(jnp.sum(widened * widened, 1), 'dp')  40.3 us
    reduce_scatter x1, waiting for transfers between devices, body(): lax.psum_scatter(partial_out, 'tensor', scatter_dimension=0, tiled=True)  32.9 us
    all_gather x1, blocking collectives, body(): lax.all_gather(attended, 'dp', axis=0, tiled=True)  23.3 us
    all_gather x1, blocking collectives, body(): normed_all = lax.all_gather(normed, 'tensor', axis=0, tiled=True)  15.3 us
    all_gather x1, blocking collectives, body(): all_rows = lax.all_gather(hidden[0], 'tensor', axis=0, tiled=True)  14.5 us
  transfers between devices with their start and end apart: 4, of which 4 were waited for; matrix products, arithmetic and copies ran while one was open for 1% of the time, Pallas kernels for 0%

commit v1 on v0

--- a/solution.py
+++ b/solution.py
@@ -8,6 +8,27 @@
 rope_theta = 500000.0
 penalty_step = 1.5
 norm_eps = 1e-05
+
+
+def gather_around(shard, axis, dim):
+    peers, index, rows = (lax.axis_size(axis), lax.axis_index(axis), shard.shape[dim])
+    upward = [(i, (i + 1) % peers) for i in range(peers)]
+    left = [(i, (i - 1) % peers) for i in range(peers)]
+    result = jnp.zeros((*shard.shape[:dim], peers * rows, *shard.shape[dim + 1 :]), shard.dtype)
+    result = lax.dynamic_update_slice_in_dim(result, shard, index * rows, axis=dim)
+    from_left = from_right = shard
+    half = peers // 2
+    for step in range(1, half + 1):
+        from_left = lax.ppermute(from_left, axis, upward)
+        result = lax.dynamic_update_slice_in_dim(
+            result, from_left, (index - step) % peers * rows, axis=dim
+        )
+        if step < peers - half:
+            from_right = lax.ppermute(from_right, axis, left)
+            result = lax.dynamic_update_slice_in_dim(
+                result, from_right, (index + step) % peers * rows, axis=dim
+            )
+    return result
 
 
 def partner_2(value, axis, distance):
@@ -121,11 +142,7 @@
     inverse = lax.rsqrt(squares / MODEL_WIDTH + norm_eps)
     normed = (widened * inverse[:, None] * norm_gain.astype(jnp.float32)).astype(jnp.bfloat16)
     normed_all = lax.all_gather(normed, "tensor", axis=0, tiled=True)
-    logits = jnp.dot(
-        lax.all_gather(normed_all, "dp", axis=1, tiled=True),
-        w_head,
-        preferred_element_type=jnp.float32,
-    )
+    logits = jnp.dot(gather_around(normed_all, "dp", 1), w_head, preferred_element_type=jnp.float32)
     stream_side = lax.axis_index("stream")
     half_rows = logits.shape[0] // 2
     mine_start = stream_side * half_rows

time: 648 us -> 671 us (1.035)
  starting transfers between devices: 0.41 us -> 42.1 us
  waiting for transfers between devices: 182 us -> 161 us
    all_gather x1 -> x0, waiting for transfers between devices: 58.3 us -> none  [body(): lax.all_gather(normed_all, 'dp', axis=1, tiled=True)]
    ppermute x0 -> x15, waiting for transfers between devices: none -> 42.3 us  [the longest x8 42 us: gather_around(): from_left = lax.ppermute(from_left, axis, upward)]
    ppermute x0 -> x15, starting transfers between devices: none -> 39 us  [the longest x7 39 us: gather_around(): from_right = lax.ppermute(from_right, axis, left)]
  transfers between devices with their start and end apart: 4 -> 18, of which waited for: 4 -> 14; matrix products, arithmetic and copies ran while one was open for 1% -> 1% of each run, Pallas kernels for 0% -> 0%
where the time goes in v1:
time: 671 us; the launch traced here: 665 us
  blocking collectives  425 us (63%)
  waiting for transfers between devices  161 us (24%)
  starting transfers between devices  42.1 us (6%)
  between operations  13.8 us (2%)
  matrix products  10.8 us (2%)
  other arithmetic  9.25 us (1%)
    psum x1, blocking collectives, body(): totals = lax.psum(jnp.sum(jnp.exp(guided), 1), ('dp', 'tensor'))  333 us
    reduce_scatter x1, waiting for transfers between devices, body(): lax.psum_scatter(jnp.concatenate([jnp.dot(all_rows, w_query, preferred_el...  80.6 us
    ppermute x8, waiting for transfers between devices, gather_around(): from_left = lax.ppermute(from_left, axis, upward)  42 us
    psum x1, blocking collectives, body(): squares = lax.psum(jnp.sum(widened * widened, 1), 'dp')  40.3 us
    ppermute x7, starting transfers between devices, gather_around(): from_right = lax.ppermute(from_right, axis, left)  39 us
    reduce_scatter x1, waiting for transfers between devices, body(): lax.psum_scatter(partial_out, 'tensor', scatter_dimension=0, tiled=True)  33 us
    all_gather x1, blocking collectives, body(): lax.all_gather(attended, 'dp', axis=0, tiled=True)  23.3 us
    all_gather x1, blocking collectives, body(): all_rows = lax.all_gather(hidden[0], 'tensor', axis=0, tiled=True)  14.5 us
  transfers between devices with their start and end apart: 18, of which 14 were waited for; matrix products, arithmetic and copies ran while one was open for 1% of the time, Pallas kernels for 0%

profile of v1, /device:TPU:128, one launch (start us, length us, event | category | flops | bytes accessed | tf_op | source)
XLA Modules:
  0.0 665.3 jit_solution(11992731392597239653)
XLA Ops:
  6.5 14.5 %all-gather = bf16[1,256,512]{2,1,0:T(8,128)(2,1)S(1)} all-gather(bf16[1,32,512]{2,1,0:T(8,128)(2,1)} %param.11), channel_id=2, replica_groups=mesh['stream'=2,'dp'=16,'tensor'=8] {'tensor'}, dimensions={1}, use_global_device_ids=true | all-gather | bytes 294912 | tf_op jit(solution)/shard_map/all_gather | solution.py:81
  24.2 80.6 %reduce-scatter.3.cloned.1.call-done = f32[16,1280]{1,0:T(8,128)} async-done(((f32[256,1280]{1,0:T(8,128)}), f32[16,1280]{1,0:T(8,128)}) %reduce-scatter.3.cloned.1.call-update) | async-done | bytes 81936 | tf_op jit(solution)/shard_map/reduce_scatter | solution.py:83
  107.9 23.3 %all_gather.10 = bf16[256,1024]{1,0:T(8,128)(2,1)S(1)} all-gather(bf16[16,1024]{1,0:T(8,128)(2,1)S(1)} %bitcast.51), channel_id=1, replica_groups=mesh['stream'=2,'dp'=16,'tensor'=8] {'dp'}, dimensions={0}, use_global_device_ids=true | all-gather | bytes 557056 | tf_op jit(solution)/shard_map/all_gather | solution.py:134
  133.7 33.0 %reduce-scatter.5.cloned.1.call-done = f32[32,512]{1,0:T(8,128)} async-done(((f32[256,512]{1,0:T(8,128)}), f32[32,512]{1,0:T(8,128)}) %reduce-scatter.5.cloned.1.call-update) | async-done | bytes 65552 | tf_op jit(solution)/shard_map/reduce_scatter | solution.py:138
  167.6 40.3 %psum.14 = f32[32]{0:T(128)S(1)} all-reduce(f32[32]{0:T(128)S(1)} %fusion.11), channel_id=1, replica_groups=mesh['stream'=2,'dp'=16,'tensor'=8] {'dp'}, use_global_device_ids=true, to_apply=%region_4.5 | all-reduce | flops 32 | bytes 256 | tf_op jit(solution)/shard_map/psum | solution.py:141
  208.8 14.2 %all_gather.11 = bf16[256,512]{1,0:T(8,128)(2,1)S(1)} all-gather(bf16[32,512]{1,0:T(8,128)(2,1)S(1)} %fusion.13), channel_id=1, replica_groups=mesh['stream'=2,'dp'=16,'tensor'=8] {'tensor'}, dimensions={0}, use_global_device_ids=true | all-gather | bytes 294912 | tf_op jit(solution)/shard_map/all_gather | solution.py:144
  223.0 5.3 collective-permute-start.1
  228.3 6.5 collective-permute-done
  234.9 5.3 collective-permute-start.3
  240.2 5.7 collective-permute-done.2
  245.9 5.4 collective-permute-start.5
  251.4 4.6 collective-permute-done.4
  256.6 5.4 collective-permute-start.7
  262.0 3.7 collective-permute-done.6
  265.9 5.8 collective-permute-start.9
  275.6 5.8 collective-permute-start.11
  281.4 3.7 collective-permute-done.10
  285.3 5.8 collective-permute-start.13
  291.2 4.6 collective-permute-done.12
  295.8 9.6 %collective-permute-done.14 = bf16[256,512]{1,0:T(8,128)(2,1)S(1)} collective-permute-done((bf16[256,512]{1,0:T(8,128)(2,1)S(1)}, bf16[256,512]{1,0:T(8,128)(2,1)S(1)}, u32[]{:S(2)}, u32[]{:S(2)}) %collective-permute-start.14) | collective-permute-done | bytes 262176 | tf_op jit(solution)/shard_map/ppermute | solution.py:22
  305.4 5.7 fusion.35
  314.2 4.6 convert_reduce_fusion
  318.9 5.5 collective-permute-done.15
  324.6 333.1 %psum.15 = f32[128]{0:T(128)S(1)} all-reduce(f32[128]{0:T(128)S(1)} %get-tuple-element.5), channel_id=1, replica_groups=mesh['stream'=2,'dp'=16,'tensor'=8] {'dp','tensor'}, use_global_device_ids=true, to_apply=%region_7.8 | all-reduce | flops 128 | bytes 1024 | tf_op jit(solution)/shard_map/psum | solution.py:160
  (87 shorter events, 19.5 us)
Async XLA Ops:
  6.5 100.5 %copy-start.1 = (bf16[1,16,1,256,128]{4,3,2,1,0:T(8,128)(2,1)S(1)}, bf16[1,16,1,256,128]{4,3,2,1,0:T(8,128)(2,1)}, u32[]{:S(2)}) copy-start(bf16[1,16,1,256,128]{4,3,2,1,0:T(8,128)(2,1)} %param.12) | copy-start | bytes 3145732
  6.5 98.3 %reduce-scatter.3.cloned.1.call-start = ((), (), s32[]{:S(2)}) async-start(), calls=%async_computation.2 | async-start | bytes 1392640 | tf_op jit(solution)/shard_map/reduce_scatter | solution.py:83
  21.1 86.5 %copy-start.2 = (bf16[1,16,1,256,128]{4,3,2,1,0:T(8,128)(2,1)S(1)}, bf16[1,16,1,256,128]{4,3,2,1,0:T(8,128)(2,1)}, u32[]{:S(2)}) copy-start(bf16[1,16,1,256,128]{4,3,2,1,0:T(8,128)(2,1)} %param.13) | copy-start | bytes 3145732
  23.9 109.7 %copy-start.5 = (bf16[512]{0:T(512)(128)(2,1)S(1)}, bf16[512]{0:T(512)(128)(2,1)}, u32[]{:S(2)}) copy-start(bf16[512]{0:T(512)(128)(2,1)} %param.20) | copy-start | bytes 3076
  23.9 142.7 %copy-start.3 = (bf16[1,32,512]{2,1,0:T(8,128)(2,1)S(1)}, bf16[1,32,512]{2,1,0:T(8,128)(2,1)}, u32[]{:S(2)}) copy-start(bf16[1,32,512]{2,1,0:T(8,128)(2,1)} %param.11) | copy-start | bytes 98308
  23.9 222.0 %copy-start.4 = (s32[256,128]{1,0:T(8,128)S(1)}, s32[256,128]{1,0:T(8,128)}, u32[]{:S(2)}) copy-start(s32[256,128]{1,0:T(8,128)} %param.15) | copy-start | bytes 393220
  23.9 227.4 %copy-start.7 = (f32[256]{0:T(256)S(1)}, f32[256]{0:T(256)}, u32[]{:S(2)}) copy-start(f32[256]{0:T(256)} %param.16) | copy-start | bytes 3076
  23.9 142.7 %reduce-scatter.5.cloned.1.call-start = ((), (), s32[]{:S(2)}) async-start(), calls=%async_computation.3 | async-start | bytes 589824 | tf_op jit(solution)/shard_map/reduce_scatter | solution.py:138
  223.0 11.9 %collective-permute-start = (bf16[256,512]{1,0:T(8,128)(2,1)S(1)}, bf16[256,512]{1,0:T(8,128)(2,1)S(1)}, u32[]{:S(2)}, u32[]{:S(2)}) collective-permute-start(bf16[256,512]{1,0:T(8,128)(2,1)S(1)} %all_gather.11), channel_id=1, source_target_pairs={{0,8},{8,16},{16,24},{24,32},{32,40},{40,48},{48,56},{56,64},{64,7... | collective-permute-start | bytes 786440 | tf_op jit(solution)/shard_map/ppermute | solution.py:22
  223.0 11.9 %collective-permute-start.1 = (bf16[256,512]{1,0:T(8,128)(2,1)S(1)}, bf16[256,512]{1,0:T(8,128)(2,1)S(1)}, u32[]{:S(2)}, u32[]{:S(2)}) collective-permute-start(bf16[256,512]{1,0:T(8,128)(2,1)S(1)} %all_gather.11), channel_id=1, source_target_pairs={{0,120},{8,0},{16,8},{24,16},{32,24},{40,32},{48,40},{56,48},{64,5... | collective-permute-start | bytes 786440 | tf_op jit(solution)/shard_map/ppermute | solution.py:27
  234.9 11.0 %collective-permute-start.2 = (bf16[256,512]{1,0:T(8,128)(2,1)S(1)}, bf16[256,512]{1,0:T(8,128)(2,1)S(1)}, u32[]{:S(2)}, u32[]{:S(2)}) collective-permute-start(bf16[256,512]{1,0:T(8,128)(2,1)S(1)} %collective-permute-done), channel_id=1, source_target_pairs={{0,8},{8,16},{16,24},{24,32},{32,40},{40,48},{48,56},{56,64},{64,7... | collective-permute-start | bytes 786440 | tf_op jit(solution)/shard_map/ppermute | solution.py:22
  234.9 11.0 %collective-permute-start.3 = (bf16[256,512]{1,0:T(8,128)(2,1)S(1)}, bf16[256,512]{1,0:T(8,128)(2,1)S(1)}, u32[]{:S(2)}, u32[]{:S(2)}) collective-permute-start(bf16[256,512]{1,0:T(8,128)(2,1)S(1)} %collective-permute-done.1), channel_id=1, source_target_pairs={{0,120},{8,0},{16,8},{24,16},{32,24},{40,32},{48,40},{56,48},{64,5... | collective-permute-start | bytes 786440 | tf_op jit(solution)/shard_map/ppermute | solution.py:27
  245.9 10.2 %collective-permute-start.4 = (bf16[256,512]{1,0:T(8,128)(2,1)S(1)}, bf16[256,512]{1,0:T(8,128)(2,1)S(1)}, u32[]{:S(2)}, u32[]{:S(2)}) collective-permute-start(bf16[256,512]{1,0:T(8,128)(2,1)S(1)} %collective-permute-done.2), channel_id=1, source_target_pairs={{0,8},{8,16},{16,24},{24,32},{32,40},{40,48},{48,56},{56,64},{64,7... | collective-permute-start | bytes 786440 | tf_op jit(solution)/shard_map/ppermute | solution.py:22
  245.9 10.7 %collective-permute-start.5 = (bf16[256,512]{1,0:T(8,128)(2,1)S(1)}, bf16[256,512]{1,0:T(8,128)(2,1)S(1)}, u32[]{:S(2)}, u32[]{:S(2)}) collective-permute-start(bf16[256,512]{1,0:T(8,128)(2,1)S(1)} %collective-permute-done.3), channel_id=1, source_target_pairs={{0,120},{8,0},{16,8},{24,16},{32,24},{40,32},{48,40},{56,48},{64,5... | collective-permute-start | bytes 786440 | tf_op jit(solution)/shard_map/ppermute | solution.py:27
  256.0 9.7 %collective-permute-start.6 = (bf16[256,512]{1,0:T(8,128)(2,1)S(1)}, bf16[256,512]{1,0:T(8,128)(2,1)S(1)}, u32[]{:S(2)}, u32[]{:S(2)}) collective-permute-start(bf16[256,512]{1,0:T(8,128)(2,1)S(1)} %collective-permute-done.4), channel_id=1, source_target_pairs={{0,8},{8,16},{16,24},{24,32},{32,40},{40,48},{48,56},{56,64},{64,7... | collective-permute-start | bytes 786440 | tf_op jit(solution)/shard_map/ppermute | solution.py:22
  256.6 9.3 %collective-permute-start.7 = (bf16[256,512]{1,0:T(8,128)(2,1)S(1)}, bf16[256,512]{1,0:T(8,128)(2,1)S(1)}, u32[]{:S(2)}, u32[]{:S(2)}) collective-permute-start(bf16[256,512]{1,0:T(8,128)(2,1)S(1)} %collective-permute-done.5), channel_id=1, source_target_pairs={{0,120},{8,0},{16,8},{24,16},{32,24},{40,32},{48,40},{56,48},{64,5... | collective-permute-start | bytes 786440 | tf_op jit(solution)/shard_map/ppermute | solution.py:27
  265.7 9.7 %collective-permute-start.8 = (bf16[256,512]{1,0:T(8,128)(2,1)S(1)}, bf16[256,512]{1,0:T(8,128)(2,1)S(1)}, u32[]{:S(2)}, u32[]{:S(2)}) collective-permute-start(bf16[256,512]{1,0:T(8,128)(2,1)S(1)} %collective-permute-done.6), channel_id=1, source_target_pairs={{0,8},{8,16},{16,24},{24,32},{32,40},{40,48},{48,56},{56,64},{64,7... | collective-permute-start | bytes 786440 | tf_op jit(solution)/shard_map/ppermute | solution.py:22
  265.9 9.7 %collective-permute-start.9 = (bf16[256,512]{1,0:T(8,128)(2,1)S(1)}, bf16[256,512]{1,0:T(8,128)(2,1)S(1)}, u32[]{:S(2)}, u32[]{:S(2)}) collective-permute-start(bf16[256,512]{1,0:T(8,128)(2,1)S(1)} %collective-permute-done.7), channel_id=1, source_target_pairs={{0,120},{8,0},{16,8},{24,16},{32,24},{40,32},{48,40},{56,48},{64,5... | collective-permute-start | bytes 786440 | tf_op jit(solution)/shard_map/ppermute | solution.py:27
  275.4 9.7 %collective-permute-start.10 = (bf16[256,512]{1,0:T(8,128)(2,1)S(1)}, bf16[256,512]{1,0:T(8,128)(2,1)S(1)}, u32[]{:S(2)}, u32[]{:S(2)}) collective-permute-start(bf16[256,512]{1,0:T(8,128)(2,1)S(1)} %collective-permute-done.8), channel_id=1, source_target_pairs={{0,8},{8,16},{16,24},{24,32},{32,40},{40,48},{48,56},{56,64},{64,7... | collective-permute-start | bytes 786440 | tf_op jit(solution)/shard_map/ppermute | solution.py:22
  275.6 9.7 %collective-permute-start.11 = (bf16[256,512]{1,0:T(8,128)(2,1)S(1)}, bf16[256,512]{1,0:T(8,128)(2,1)S(1)}, u32[]{:S(2)}, u32[]{:S(2)}) collective-permute-start(bf16[256,512]{1,0:T(8,128)(2,1)S(1)} %collective-permute-done.9), channel_id=1, source_target_pairs={{0,120},{8,0},{16,8},{24,16},{32,24},{40,32},{48,40},{56,48},{64,5... | collective-permute-start | bytes 786440 | tf_op jit(solution)/shard_map/ppermute | solution.py:27
  285.1 10.6 %collective-permute-start.12 = (bf16[256,512]{1,0:T(8,128)(2,1)S(1)}, bf16[256,512]{1,0:T(8,128)(2,1)S(1)}, u32[]{:S(2)}, u32[]{:S(2)}) collective-permute-start(bf16[256,512]{1,0:T(8,128)(2,1)S(1)} %collective-permute-done.10), channel_id=1, source_target_pairs={{0,8},{8,16},{16,24},{24,32},{32,40},{40,48},{48,56},{56,64},{64,7... | collective-permute-start | bytes 786440 | tf_op jit(solution)/shard_map/ppermute | solution.py:22
  285.3 10.5 %collective-permute-start.13 = (bf16[256,512]{1,0:T(8,128)(2,1)S(1)}, bf16[256,512]{1,0:T(8,128)(2,1)S(1)}, u32[]{:S(2)}, u32[]{:S(2)}) collective-permute-start(bf16[256,512]{1,0:T(8,128)(2,1)S(1)} %collective-permute-done.11), channel_id=1, source_target_pairs={{0,120},{8,0},{16,8},{24,16},{32,24},{40,32},{48,40},{56,48},{64,5... | collective-permute-start | bytes 786440 | tf_op jit(solution)/shard_map/ppermute | solution.py:27
  295.7 9.7 %collective-permute-start.14 = (bf16[256,512]{1,0:T(8,128)(2,1)S(1)}, bf16[256,512]{1,0:T(8,128)(2,1)S(1)}, u32[]{:S(2)}, u32[]{:S(2)}) collective-permute-start(bf16[256,512]{1,0:T(8,128)(2,1)S(1)} %collective-permute-done.12), channel_id=1, source_target_pairs={{0,8},{8,16},{16,24},{24,32},{32,40},{40,48},{48,56},{56,64},{64,7... | collective-permute-start | bytes 786440 | tf_op jit(solution)/shard_map/ppermute | solution.py:22
  311.2 13.2 %collective-permute-start.15 = (f32[128,512]{1,0:T(8,128)S(1)}, f32[128,512]{1,0:T(8,128)S(1)}, u32[]{:S(2)}, u32[]{:S(2)}) collective-permute-start(f32[128,512]{1,0:T(8,128)S(1)} %constant_dynamic-slice_fusion.1), channel_id=1, source_target_pairs={{0,128},{128,0},{1,129},{129,1},{2,130},{130,2},{3,131},{131,3},{4... | collective-permute-start | bytes 786440 | tf_op jit(solution)/shard_map/ppermute | solution.py:37
  (2 other events, 32.0 us)
Sparse Core Ops, SparseCore 0:
  24.1 80.7 reduce-scatter.2
  133.8 32.8 reduce-scatter.4
